TPU v7x, 32 devices: a whole 2x2x4 slice. The times are simulated.
32 devices in a mesh: locus: 2 (over x), row: 4 (over y, core), col: 4 (over z).
Axes of the slice: x: 2, y: 2, z: 4, core: 2. Of those that a mesh axis runs over, the one named last changes fastest.
Arguments:
- input_map: bfloat16 [192, 96, 128], P(('locus', 'row'), 'col'), parts along dimension 0, may hold values from -6 to 6
- conv_weights: bfloat16 [2, 4, 3, 3, 128, 128], replicated, may hold values from -0.25 to 0.25
- conv_bias: float32 [2, 4, 128], replicated, may hold values from -3 to 3
Outputs:
- contact_map: bfloat16 [192, 96, 128], P(('locus', 'row'), 'col'), parts along dimension 0
There are 2 independent parts, one for each index of `locus`. A program takes and returns all parts, laid end to end along the dimension named above; an argument that names none is the same for every part. Nothing has to cross between parts.
All inputs are finite; a program needn't handle non-finite values.
Results may differ from a plain program's by a relative error of at most 0.012.
Values may be sent and summed in bfloat16 or wider, within the bound.
A program may use at most 64 MiB of HBM per device.

v0:
```python
import jax
import jax.numpy as jnp
from jax import lax
from jax.sharding import PartitionSpec as P

GROUPS = 2
LAYERS = 4


def extended(cells, sides, width):
    for axis, dim in sides:
        count = lax.axis_size(axis)
        ends = count - 1
        head = lax.slice_in_dim(cells, 0, width, axis=dim)
        tail = lax.slice_in_dim(cells, cells.shape[dim] - width, cells.shape[dim], axis=dim)
        cells = jnp.concatenate(
            [
                lax.ppermute(tail, axis, [(i, (i + 1) % count) for i in range(ends)]),
                cells,
                lax.ppermute(head, axis, [((i + 1) % count, i) for i in range(ends)]),
            ],
            axis=dim,
        )
    return cells


def convolve(padded, weight, bias_row, dilation):
    summed = lax.conv_general_dilated(
        padded[None],
        weight,
        (1, 1),
        "VALID",
        rhs_dilation=(dilation, dilation),
        dimension_numbers=("NHWC", "HWIO", "NHWC"),
        preferred_element_type=jnp.float32,
    )[0]
    return jax.nn.relu(summed + bias_row)


def mirror_axes(tile):
    row_count = lax.axis_size("row")
    col_count = lax.axis_size("col")
    fine_size = tile.shape[0] // col_count
    channels = tile.shape[2]
    ratio = row_count // col_count
    blocks = tile.reshape(col_count, fine_size, row_count, fine_size, channels)
    first_pass = lax.all_to_all(blocks, "col", split_axis=0, concat_axis=0, tiled=True)
    reordered = jnp.transpose(first_pass, (0, 2, 1, 3, 4)).reshape(
        row_count, col_count, fine_size, fine_size, channels
    )
    second = lax.all_to_all(reordered, "row", split_axis=0, concat_axis=0, tiled=True)
    second = second.reshape(col_count, ratio, col_count, fine_size, fine_size, channels)
    third_pass = lax.all_to_all(second, "col", split_axis=0, concat_axis=0, tiled=True)
    return jnp.transpose(third_pass, (2, 4, 1, 0, 3, 5)).reshape(
        col_count * fine_size, row_count * fine_size, channels
    )


def body(input_map, conv_weights, conv_bias):
    tile_rows = input_map.shape[0]
    tile_cols = input_map.shape[1]
    row_start = lax.axis_index("row") * tile_rows
    col_start = lax.axis_index("col") * tile_cols
    total_rows = tile_rows * lax.axis_size("row")
    total_cols = tile_cols * lax.axis_size("col")
    carried = input_map
    for group_idx in range(GROUPS):
        margin = 2**LAYERS - 1
        hidden = extended(carried, (("row", 0), ("col", 1)), margin)
        for layer_idx in range(LAYERS):
            dilation = 2**layer_idx
            margin = margin - dilation
            active = convolve(
                hidden,
                conv_weights[group_idx, layer_idx],
                conv_bias[group_idx, layer_idx],
                dilation,
            )
            row_pos = row_start - margin + jnp.arange(active.shape[0], dtype=jnp.int32)
            col_pos = col_start - margin + jnp.arange(active.shape[1], dtype=jnp.int32)
            row_ok = (row_pos >= 0) & (row_pos < total_rows)
            col_ok = (col_pos >= 0) & (col_pos < total_cols)
            inside = row_ok[:, None, None] & col_ok[None, :, None]
            hidden = jnp.where(inside, active, 0.0).astype(jnp.bfloat16)
        carried = (carried.astype(jnp.float32) + hidden.astype(jnp.float32)).astype(jnp.bfloat16)
    mirrored = mirror_axes(carried)
    return (0.5 * (carried.astype(jnp.float32) + mirrored.astype(jnp.float32))).astype(jnp.bfloat16)


def solution(mesh):
    placed = (P(("locus", "row"), "col", None), P(), P())
    return jax.shard_map(
        body,
        mesh=mesh,
        in_specs=placed,
        out_specs=P(("locus", "row"), "col", None),
        check_vma=False,
    )
```

profile of v0, /device:TPU:0, one launch (start us, length us, event | category | flops | bytes accessed | tf_op | source)
XLA Modules:
  0.0 99.5 jit_solution(8267892050423417603)
XLA Ops:
  0.0 1.0 fusion.77
  1.0 1.3 %collective-permute-start.1 = (bf16[15,24,128]{2,1,0:T(8,128)(2,1)S(1)}, bf16[15,24,128]{2,1,0:T(8,128)(2,1)S(1)}, u32[]{:S(2)}, u32[]{:S(2)}) collective-permute-start(bf16[15,24,128]{2,1,0:T(8,128)(2,1)S(1)} %get-tuple-element.11), channel_id=1, source_target_pairs={{4,0},{8,4},{12,8},{5,1},{9,5},{13,9},{6,2},{10,6},{14,10},{7,3},{... | collective-permute-start | bytes 276488 | tf_op jit(solution)/shard_map/ppermute | solution.py:20
  2.3 3.0 %collective-permute-start = (bf16[15,24,128]{2,1,0:T(8,128)(2,1)S(1)}, bf16[15,24,128]{2,1,0:T(8,128)(2,1)S(1)}, u32[]{:S(2)}, u32[]{:S(2)}) collective-permute-start(bf16[15,24,128]{2,1,0:T(8,128)(2,1)S(1)} %get-tuple-element.12), channel_id=1, source_target_pairs={{0,4},{4,8},{8,12},{1,5},{5,9},{9,13},{2,6},{6,10},{10,14},{3,7},{... | collective-permute-start | bytes 276488 | tf_op jit(solution)/shard_map/ppermute | solution.py:18
  5.3 0.9 slice_bitcast_fusion.10
  6.5 0.9 constant_dynamic-update-slice_fusion.1
  7.6 5.0 %collective-permute-start.2 = (bf16[54,15,128]{2,1,0:T(8,128)(2,1)S(1)}, bf16[54,15,128]{2,1,0:T(8,128)(2,1)S(1)}, u32[]{:S(2)}, u32[]{:S(2)}) collective-permute-start(bf16[54,15,128]{2,1,0:T(8,128)(2,1)S(1)} %get-tuple-element.7), channel_id=1, source_target_pairs={{0,1},{1,2},{2,3},{4,5},{5,6},{6,7},{8,9},{9,10},{10,11},{12,13},{... | collective-permute-start | bytes 622088 | tf_op jit(solution)/shard_map/ppermute | solution.py:18
  12.6 1.3 %collective-permute-start.3 = (bf16[54,15,128]{2,1,0:T(8,128)(2,1)S(1)}, bf16[54,15,128]{2,1,0:T(8,128)(2,1)S(1)}, u32[]{:S(2)}, u32[]{:S(2)}) collective-permute-start(bf16[54,15,128]{2,1,0:T(8,128)(2,1)S(1)} %get-tuple-element.8), channel_id=1, source_target_pairs={{1,0},{2,1},{3,2},{5,4},{6,5},{7,6},{9,8},{10,9},{11,10},{13,12},{... | collective-permute-start | bytes 622088 | tf_op jit(solution)/shard_map/ppermute | solution.py:20
  14.0 3.9 %collective-permute-done.2 = bf16[54,15,128]{2,1,0:T(8,128)(2,1)S(1)} collective-permute-done((bf16[54,15,128]{2,1,0:T(8,128)(2,1)S(1)}, bf16[54,15,128]{2,1,0:T(8,128)(2,1)S(1)}, u32[]{:S(2)}, u32[]{:S(2)}) %collective-permute-start.2) | collective-permute-done | bytes 207392 | tf_op jit(solution)/shard_map/ppermute | solution.py:18
  17.8 4.7 %collective-permute-done.3 = bf16[54,15,128]{2,1,0:T(8,128)(2,1)S(1)} collective-permute-done((bf16[54,15,128]{2,1,0:T(8,128)(2,1)S(1)}, bf16[54,15,128]{2,1,0:T(8,128)(2,1)S(1)}, u32[]{:S(2)}, u32[]{:S(2)}) %collective-permute-start.3) | collective-permute-done | bytes 207392 | tf_op jit(solution)/shard_map/ppermute | solution.py:20
  22.5 0.3 maximum_bitcast_fusion
  22.8 0.1 copy.48
  23.0 0.1 copy.28
  23.2 0.4 copy-done.2
  23.6 2.9 %add_maximum_fusion.1 = bf16[52,8,7,128]{3,1,2,0:T(8,128)(2,1)S(1)} fusion(bf16[54,1,7,2,128]{4,2,3,0,1:T(8,128)(2,1)S(1)} %slice.106, bf16[54,1,8,7,128]{4,2,3,0,1:T(8,128)(2,1)S(1)} %copy.28, f32[128]{0:T(128)S(1)} %get-tuple-element.19, pred[8,7]{0,1:T(8,128)(4,1)S(1)} %copy-done.2, bf16[2,4,3,3,128,128]{5,4,3,2,1,0:T(8,128)(2,1)} %param.4), kind=kOutput, calls=%fused_computation.13 | convolution fusion | flops 863260672 | bytes 2008632 | tf_op jit(solution)/shard_map/conv_general_dilated | solution.py:28
  26.5 0.1 copy.29
  26.6 0.7 fusion.5
  27.4 0.1 copy.31
  27.5 0.1 slice.108
  27.6 0.4 copy-done.1
  28.0 2.7 %add_maximum_fusion.3 = bf16[48,8,7,128]{3,1,2,0:T(8,128)(2,1)S(1)} fusion(bf16[52,1,7,4,128]{4,2,3,0,1:T(8,128)(2,1)S(1)} %slice.108, bf16[52,1,8,7,128]{4,2,3,0,1:T(8,128)(2,1)S(1)} %copy.31, f32[128]{0:T(128)S(1)} %get-tuple-element.18, pred[8,7]{0,1:T(8,128)(4,1)S(1)} %copy-done.1, bf16[2,4,3,3,128,128]{5,4,3,2,1,0:T(8,128)(2,1)} %param.4), kind=kOutput, calls=%fused_computation.17 | convolution fusion | flops 797614080 | bytes 2101816 | tf_op jit(solution)/shard_map/conv_general_dilated | solution.py:28
  30.8 0.1 copy.32
  30.9 0.5 fusion.42
  31.4 6.8 %fusion.8 = f32[1,24,24,128]{3,0,2,1:T(1,128)S(1)} fusion(pred[40,40]{1,0:T(8,128)(4,1)S(1)} %broadcast_and_fusion.2, bf16[1,48,48,128]{3,1,2,0:T(8,128)(2,1)S(1)} %fusion.42, f32[128]{0:T(128)S(1)} %get-tuple-element.17, bf16[2,4,3,3,128,128]{5,4,3,2,1,0:T(8,128)(2,1)} %param.4), kind=kOutput, calls=%fused_computation.22 | convolution fusion | flops 642547712 | bytes 1476672 | tf_op jit(solution)/shard_map/conv_general_dilated | solution.py:28
  38.2 0.1 add_convert_fusion.1
  38.3 2.0 %collective-permute-start.4 = (bf16[15,24,128]{2,1,0:T(8,128)(2,1)S(1)}, bf16[15,24,128]{2,1,0:T(8,128)(2,1)S(1)}, u32[]{:S(2)}, u32[]{:S(2)}) collective-permute-start(bf16[15,24,128]{2,1,0:T(8,128)(2,1)S(1)} %get-tuple-element.9), channel_id=1, source_target_pairs={{0,4},{4,8},{8,12},{1,5},{5,9},{9,13},{2,6},{6,10},{10,14},{3,7},{... | collective-permute-start | bytes 276488 | tf_op jit(solution)/shard_map/ppermute | solution.py:18
  40.4 1.5 %collective-permute-start.5 = (bf16[15,24,128]{2,1,0:T(8,128)(2,1)S(1)}, bf16[15,24,128]{2,1,0:T(8,128)(2,1)S(1)}, u32[]{:S(2)}, u32[]{:S(2)}) collective-permute-start(bf16[15,24,128]{2,1,0:T(8,128)(2,1)S(1)} %get-tuple-element.10), channel_id=1, source_target_pairs={{4,0},{8,4},{12,8},{5,1},{9,5},{13,9},{6,2},{10,6},{14,10},{7,3},{... | collective-permute-start | bytes 276488 | tf_op jit(solution)/shard_map/ppermute | solution.py:20
  41.9 2.9 %collective-permute-done.5 = bf16[15,24,128]{2,1,0:T(8,128)(2,1)S(1)} collective-permute-done((bf16[15,24,128]{2,1,0:T(8,128)(2,1)S(1)}, bf16[15,24,128]{2,1,0:T(8,128)(2,1)S(1)}, u32[]{:S(2)}, u32[]{:S(2)}) %collective-permute-start.5) | collective-permute-done | bytes 92192 | tf_op jit(solution)/shard_map/ppermute | solution.py:20
  44.9 3.5 %collective-permute-start.6 = (bf16[54,15,128]{2,1,0:T(8,128)(2,1)S(1)}, bf16[54,15,128]{2,1,0:T(8,128)(2,1)S(1)}, u32[]{:S(2)}, u32[]{:S(2)}) collective-permute-start(bf16[54,15,128]{2,1,0:T(8,128)(2,1)S(1)} %get-tuple-element.5), channel_id=1, source_target_pairs={{0,1},{1,2},{2,3},{4,5},{5,6},{6,7},{8,9},{9,10},{10,11},{12,13},{... | collective-permute-start | bytes 622088 | tf_op jit(solution)/shard_map/ppermute | solution.py:18
  48.4 1.3 %collective-permute-start.7 = (bf16[54,15,128]{2,1,0:T(8,128)(2,1)S(1)}, bf16[54,15,128]{2,1,0:T(8,128)(2,1)S(1)}, u32[]{:S(2)}, u32[]{:S(2)}) collective-permute-start(bf16[54,15,128]{2,1,0:T(8,128)(2,1)S(1)} %get-tuple-element.6), channel_id=1, source_target_pairs={{1,0},{2,1},{3,2},{5,4},{6,5},{7,6},{9,8},{10,9},{11,10},{13,12},{... | collective-permute-start | bytes 622088 | tf_op jit(solution)/shard_map/ppermute | solution.py:20
  49.7 2.3 %collective-permute-done.6 = bf16[54,15,128]{2,1,0:T(8,128)(2,1)S(1)} collective-permute-done((bf16[54,15,128]{2,1,0:T(8,128)(2,1)S(1)}, bf16[54,15,128]{2,1,0:T(8,128)(2,1)S(1)}, u32[]{:S(2)}, u32[]{:S(2)}) %collective-permute-start.6) | collective-permute-done | bytes 207392 | tf_op jit(solution)/shard_map/ppermute | solution.py:18
  52.0 4.7 %collective-permute-done.7 = bf16[54,15,128]{2,1,0:T(8,128)(2,1)S(1)} collective-permute-done((bf16[54,15,128]{2,1,0:T(8,128)(2,1)S(1)}, bf16[54,15,128]{2,1,0:T(8,128)(2,1)S(1)}, u32[]{:S(2)}, u32[]{:S(2)}) %collective-permute-start.7) | collective-permute-done | bytes 207392 | tf_op jit(solution)/shard_map/ppermute | solution.py:20
  56.6 0.3 maximum_bitcast_fusion.1
  56.9 0.1 copy.49
  57.1 0.1 copy.36
  57.3 2.9 %add_maximum_fusion = bf16[52,8,7,128]{3,1,2,0:T(8,128)(2,1)S(1)} fusion(bf16[54,1,7,2,128]{4,2,3,0,1:T(8,128)(2,1)S(1)} %slice.114, bf16[54,1,8,7,128]{4,2,3,0,1:T(8,128)(2,1)S(1)} %copy.36, f32[128]{0:T(128)S(1)} %get-tuple-element.15, pred[8,7]{0,1:T(8,128)(4,1)S(1)} %copy-done.2, bf16[2,4,3,3,128,128]{5,4,3,2,1,0:T(8,128)(2,1)} %param.4), kind=kOutput, calls=%fused_computation.12 | convolution fusion | flops 863260672 | bytes 2008632 | tf_op jit(solution)/shard_map/conv_general_dilated | solution.py:28
  60.2 0.1 copy.37
  60.3 0.7 fusion.4
  61.0 0.1 copy.39
  61.2 0.1 slice.116
  61.3 2.7 %add_maximum_fusion.2 = bf16[48,8,7,128]{3,1,2,0:T(8,128)(2,1)S(1)} fusion(bf16[52,1,7,4,128]{4,2,3,0,1:T(8,128)(2,1)S(1)} %slice.116, bf16[52,1,8,7,128]{4,2,3,0,1:T(8,128)(2,1)S(1)} %copy.39, f32[128]{0:T(128)S(1)} %get-tuple-element.14, pred[8,7]{0,1:T(8,128)(4,1)S(1)} %copy-done.1, bf16[2,4,3,3,128,128]{5,4,3,2,1,0:T(8,128)(2,1)} %param.4), kind=kOutput, calls=%fused_computation.16 | convolution fusion | flops 797614080 | bytes 2101816 | tf_op jit(solution)/shard_map/conv_general_dilated | solution.py:28
  64.0 0.1 copy.40
  64.1 0.5 fusion.43
  64.6 6.7 %fusion.11 = f32[1,24,24,128]{3,0,2,1:T(1,128)S(1)} fusion(pred[40,40]{1,0:T(8,128)(4,1)S(1)} %broadcast_and_fusion.2, bf16[1,48,48,128]{3,1,2,0:T(8,128)(2,1)S(1)} %fusion.43, f32[128]{0:T(128)S(1)} %get-tuple-element.20, bf16[2,4,3,3,128,128]{5,4,3,2,1,0:T(8,128)(2,1)} %param.4), kind=kOutput, calls=%fused_computation.25 | convolution fusion | flops 642547712 | bytes 1476672 | tf_op jit(solution)/shard_map/conv_general_dilated | solution.py:28
  71.4 0.1 add_convert_fusion
  71.6 9.9 %all_to_all.15 = bf16[4,6,4,6,128]{4,2,3,1,0:T(4,128)(2,1)S(1)} all-to-all(bf16[4,6,4,6,128]{4,2,3,1,0:T(4,128)(2,1)S(1)} %copy.43), channel_id=1, replica_groups=mesh['locus'=2,'row'=4,'col'=4] {'col'}, dimensions={0} | all-to-all | bytes 294912 | tf_op jit(solution)/shard_map/all_to_all | solution.py:47
  81.5 7.8 %all_to_all.16 = bf16[4,4,6,6,128]{4,1,3,2,0:T(4,128)(2,1)S(1)} all-to-all(bf16[4,4,6,6,128]{4,1,3,2,0:T(4,128)(2,1)S(1)} %bitcast.88), channel_id=1, replica_groups=mesh['locus'=2,'row'=4,'col'=4] {'row'}, dimensions={0} | all-to-all | bytes 294912 | tf_op jit(solution)/shard_map/all_to_all | solution.py:51
  89.3 9.3 %all_to_all.17 = bf16[4,1,4,6,6,128]{5,2,4,3,1,0:T(4,128)(2,1)S(1)} all-to-all(bf16[4,1,4,6,6,128]{5,2,4,3,1,0:T(4,128)(2,1)S(1)} %bitcast.89), channel_id=1, replica_groups=mesh['locus'=2,'row'=4,'col'=4] {'col'}, dimensions={0} | all-to-all | bytes 294912 | tf_op jit(solution)/shard_map/all_to_all | solution.py:53
  98.8 0.7 multiply_convert_fusion
  (32 shorter events, 1.3 us)
Async XLA Ops:
  1.0 6.5 %collective-permute-start.1 = (bf16[15,24,128]{2,1,0:T(8,128)(2,1)S(1)}, bf16[15,24,128]{2,1,0:T(8,128)(2,1)S(1)}, u32[]{:S(2)}, u32[]{:S(2)}) collective-permute-start(bf16[15,24,128]{2,1,0:T(8,128)(2,1)S(1)} %get-tuple-element.11), channel_id=1, source_target_pairs={{4,0},{8,4},{12,8},{5,1},{9,5},{13,9},{6,2},{10,6},{14,10},{7,3},{... | collective-permute-start | bytes 276488 | tf_op jit(solution)/shard_map/ppermute | solution.py:20
  2.3 4.2 %collective-permute-start = (bf16[15,24,128]{2,1,0:T(8,128)(2,1)S(1)}, bf16[15,24,128]{2,1,0:T(8,128)(2,1)S(1)}, u32[]{:S(2)}, u32[]{:S(2)}) collective-permute-start(bf16[15,24,128]{2,1,0:T(8,128)(2,1)S(1)} %get-tuple-element.12), channel_id=1, source_target_pairs={{0,4},{4,8},{8,12},{1,5},{5,9},{9,13},{2,6},{6,10},{10,14},{3,7},{... | collective-permute-start | bytes 276488 | tf_op jit(solution)/shard_map/ppermute | solution.py:18
  7.6 10.2 %collective-permute-start.2 = (bf16[54,15,128]{2,1,0:T(8,128)(2,1)S(1)}, bf16[54,15,128]{2,1,0:T(8,128)(2,1)S(1)}, u32[]{:S(2)}, u32[]{:S(2)}) collective-permute-start(bf16[54,15,128]{2,1,0:T(8,128)(2,1)S(1)} %get-tuple-element.7), channel_id=1, source_target_pairs={{0,1},{1,2},{2,3},{4,5},{5,6},{6,7},{8,9},{9,10},{10,11},{12,13},{... | collective-permute-start | bytes 622088 | tf_op jit(solution)/shard_map/ppermute | solution.py:18
  12.6 9.9 %collective-permute-start.3 = (bf16[54,15,128]{2,1,0:T(8,128)(2,1)S(1)}, bf16[54,15,128]{2,1,0:T(8,128)(2,1)S(1)}, u32[]{:S(2)}, u32[]{:S(2)}) collective-permute-start(bf16[54,15,128]{2,1,0:T(8,128)(2,1)S(1)} %get-tuple-element.8), channel_id=1, source_target_pairs={{1,0},{2,1},{3,2},{5,4},{6,5},{7,6},{9,8},{10,9},{11,10},{13,12},{... | collective-permute-start | bytes 622088 | tf_op jit(solution)/shard_map/ppermute | solution.py:20
  22.9 0.7 copy-start.2
  27.4 0.7 copy-start.1
  31.4 6.8 %copy-start = (bf16[24,24,128]{2,1,0:T(8,128)(2,1)S(1)}, bf16[24,24,128]{2,1,0:T(8,128)(2,1)}, u32[]{:S(2)}) copy-start(bf16[24,24,128]{2,1,0:T(8,128)(2,1)} %param.3) | copy-start | bytes 442372
  38.3 3.5 %collective-permute-start.4 = (bf16[15,24,128]{2,1,0:T(8,128)(2,1)S(1)}, bf16[15,24,128]{2,1,0:T(8,128)(2,1)S(1)}, u32[]{:S(2)}, u32[]{:S(2)}) collective-permute-start(bf16[15,24,128]{2,1,0:T(8,128)(2,1)S(1)} %get-tuple-element.9), channel_id=1, source_target_pairs={{0,4},{4,8},{8,12},{1,5},{5,9},{9,13},{2,6},{6,10},{10,14},{3,7},{... | collective-permute-start | bytes 276488 | tf_op jit(solution)/shard_map/ppermute | solution.py:18
  40.4 4.4 %collective-permute-start.5 = (bf16[15,24,128]{2,1,0:T(8,128)(2,1)S(1)}, bf16[15,24,128]{2,1,0:T(8,128)(2,1)S(1)}, u32[]{:S(2)}, u32[]{:S(2)}) collective-permute-start(bf16[15,24,128]{2,1,0:T(8,128)(2,1)S(1)} %get-tuple-element.10), channel_id=1, source_target_pairs={{4,0},{8,4},{12,8},{5,1},{9,5},{13,9},{6,2},{10,6},{14,10},{7,3},{... | collective-permute-start | bytes 276488 | tf_op jit(solution)/shard_map/ppermute | solution.py:20
  44.9 7.1 %collective-permute-start.6 = (bf16[54,15,128]{2,1,0:T(8,128)(2,1)S(1)}, bf16[54,15,128]{2,1,0:T(8,128)(2,1)S(1)}, u32[]{:S(2)}, u32[]{:S(2)}) collective-permute-start(bf16[54,15,128]{2,1,0:T(8,128)(2,1)S(1)} %get-tuple-element.5), channel_id=1, source_target_pairs={{0,1},{1,2},{2,3},{4,5},{5,6},{6,7},{8,9},{9,10},{10,11},{12,13},{... | collective-permute-start | bytes 622088 | tf_op jit(solution)/shard_map/ppermute | solution.py:18
  48.4 8.3 %collective-permute-start.7 = (bf16[54,15,128]{2,1,0:T(8,128)(2,1)S(1)}, bf16[54,15,128]{2,1,0:T(8,128)(2,1)S(1)}, u32[]{:S(2)}, u32[]{:S(2)}) collective-permute-start(bf16[54,15,128]{2,1,0:T(8,128)(2,1)S(1)} %get-tuple-element.6), channel_id=1, source_target_pairs={{1,0},{2,1},{3,2},{5,4},{6,5},{7,6},{9,8},{10,9},{11,10},{13,12},{... | collective-permute-start | bytes 622088 | tf_op jit(solution)/shard_map/ppermute | solution.py:20
where the time goes:
time: 100 us; the launch traced here: 99.5 us
  blocking collectives  27 us (27%)
  matrix products  24.7 us (25%)
  starting transfers between devices  18.9 us (19%)
  waiting for transfers between devices  18.4 us (18%)
  local copies, waits for them, and re-layouts  5.77 us (6%)
  other arithmetic  4.25 us (4%)
    conv_general_dilated x6, matrix products, convolve(): lax.conv_general_dilated(padded[None], weight, (1, 1), 'VALID', rhs_dilat...  24.7 us
    ppermute x4, starting transfers between devices, extended(): lax.ppermute(tail, axis, [(i, (i + 1) % count) for i in range(ends)])  13.5 us
    ppermute x4, waiting for transfers between devices, extended(): lax.ppermute(head, axis, [((i + 1) % count, i) for i in range(ends)])  12.2 us
    all_to_all x1, blocking collectives, mirror_axes(): lax.all_to_all(blocks, 'col', split_axis=0, concat_axis=0, tiled=True)  9.89 us
    all_to_all x1, blocking collectives, mirror_axes(): lax.all_to_all(second, 'col', split_axis=0, concat_axis=0, tiled=True)  9.29 us
    all_to_all x1, blocking collectives, mirror_axes(): lax.all_to_all(reordered, 'row', split_axis=0, concat_axis=0, tiled=True)  7.81 us
    ppermute x4, waiting for transfers between devices, extended(): lax.ppermute(tail, axis, [(i, (i + 1) % count) for i in range(ends)])  6.16 us
    ppermute x4, starting transfers between devices, extended(): lax.ppermute(head, axis, [((i + 1) % count, i) for i in range(ends)])  5.35 us
  transfers between devices with their start and end apart: 8, of which 5 were waited for; matrix products, arithmetic and copies ran while one was open for 2% of the time, Pallas kernels for 0%

commit v1 on v0

v1 whole, which is shorter than its diff:
```python
import functools

import jax
import jax.numpy as jnp
from jax import lax
from jax.experimental import pallas as pl
from jax.experimental.pallas import tpu as pltpu
from jax.sharding import PartitionSpec as P

SEGMENTS = ((0, 1, 2, 3),)
PAD = 16
CHUNK_ROWS = 832
MESH = pl.DeviceIdType.MESH


def round_up(value, unit):
    return -(-value // unit) * unit


def neighbours():
    return [(dr, dc) for dr in (-1, 0, 1) for dc in (-1, 0, 1) if (dr, dc) != (0, 0)]


def slot_of(dr, dc):
    return (dr + 1) * 3 + (dc + 1)


def trunk(
    shape, plan, rows_n, cols_n,
    input_ref, weight_ref, bias_ref, out_ref,
    taps, acts, own, edge, side, cap, corner, mir_send, mir_recv,
    weight_sem, input_sem, halo_send, halo_recv, mir_sems, mir_rsems, mir_local,
):
    groups, layers, tile_rows, tile_cols = shape
    ratio = rows_n // cols_n
    row = lax.axis_index("row")
    col = lax.axis_index("col")
    width = acts.shape[3]
    row_start = row * tile_rows
    col_start = col * tile_cols

    copies = []
    for k in range(groups * layers):
        for o in range(2):
            cp = pltpu.make_async_copy(
                weight_ref.at[k // layers, k % layers],
                taps.at[k, pl.ds(o, 3), :, :, pl.ds(o * 128, 128)],
                weight_sem.at[k, o],
            )
            copies.append(cp)
    load = pltpu.make_async_copy(input_ref, own.at[0], input_sem)
    load.start()
    for cp in copies:
        cp.start()

    side[...] = jnp.zeros_like(side)
    cap[...] = jnp.zeros_like(cap)
    corner[...] = jnp.zeros_like(corner)

    def exists(dr, dc):
        ok = jnp.bool_(True)
        if dr:
            ok = jnp.logical_and(ok, (row > 0) if dr < 0 else (row < rows_n - 1))
        if dc:
            ok = jnp.logical_and(ok, (col > 0) if dc < 0 else (col < cols_n - 1))
        return ok

    def device(dr, dc):
        return {"row": row + dr, "col": col + dc}

    partners = []
    for s in range(ratio):
        peer_row = ratio * col + s
        peer_col = row // ratio
        same = jnp.logical_and(peer_row == row, peer_col == col)
        partners.append((peer_row, peer_col, same))

    barrier = pltpu.get_barrier_semaphore()
    for dr, dc in neighbours():
        @pl.when(exists(dr, dc))
        def _():
            pl.semaphore_signal(barrier, inc=1, device_id=device(dr, dc), device_id_type=MESH)
    for peer_row, peer_col, same in partners:
        @pl.when(jnp.logical_not(same))
        def _():
            pl.semaphore_signal(
                barrier, inc=1, device_id={"row": peer_row, "col": peer_col}, device_id_type=MESH
            )

    acts[...] = jnp.zeros_like(acts)
    taps[:, 3, :, :, 0:128] = jnp.zeros((groups * layers, 3, 128, 128), jnp.bfloat16)
    taps[:, 0, :, :, 128:256] = jnp.zeros((groups * layers, 3, 128, 128), jnp.bfloat16)

    load.wait()

    def stage_edges(seg, margin, reach):
        value = own[seg].astype(jnp.float32)
        edge[seg, 0, :, :reach, :] = value[:, :reach, :].astype(jnp.bfloat16)
        edge[seg, 1, :, :reach, :] = value[:, tile_cols - reach :, :].astype(jnp.bfloat16)

    def transfer(seg, margin, reach, dr, dc):
        low = pl.ds(0, margin)
        high = pl.ds(tile_rows - margin, margin)
        rows = low if dr < 0 else high
        if dc == 0:
            src = own.at[seg, rows]
            dst = cap.at[seg, 1 if dr < 0 else 0, pl.ds(0, margin)]
        elif dr == 0:
            src = edge.at[seg, 0 if dc < 0 else 1, :, pl.ds(0, reach)]
            dst = side.at[seg, 1 if dc < 0 else 0, :, pl.ds(0, reach)]
        else:
            src = edge.at[seg, 0 if dc < 0 else 1, rows, pl.ds(0, reach)]
            dst = corner.at[
                seg, 1 if dr < 0 else 0, 1 if dc < 0 else 0, pl.ds(0, margin), pl.ds(0, reach)
            ]
        return pltpu.make_async_remote_copy(
            src_ref=src,
            dst_ref=dst,
            send_sem=halo_send.at[seg, slot_of(dr, dc)],
            recv_sem=halo_recv.at[seg, slot_of(-dr, -dc)],
            device_id=device(dr, dc),
            device_id_type=MESH,
        )

    def arrive(seg, margin, reach, dr, dc):
        transfer(seg, margin, reach, -dr, -dc).wait_recv()

    order = [(0, -1), (0, 1), (-1, 0), (1, 0), (-1, -1), (-1, 1), (1, -1), (1, 1)]

    def send_halo(seg, margin, reach):
        for dr, dc in order:
            @pl.when(exists(dr, dc))
            def _():
                transfer(seg, margin, reach, dr, dc).start()

    def wait_halo(seg, margin, reach):
        for dr, dc in order:
            @pl.when(exists(dr, dc))
            def _():
                arrive(seg, margin, reach, dr, dc)

    def wait_sent(seg, margin, reach):
        for dr, dc in order:
            @pl.when(exists(dr, dc))
            def _():
                transfer(seg, margin, reach, dr, dc).wait_send()

    def spread(buf, at, start, span, value, dilation):
        acts[buf, 1, at, pl.ds(start, span), :] = value.astype(jnp.bfloat16)
        acts[buf, 0, at, pl.ds(start, span), :] = pltpu.roll(value, dilation, 0).astype(jnp.bfloat16)
        acts[buf, 2, at, pl.ds(start, span), :] = pltpu.roll(value, span - dilation, 0).astype(
            jnp.bfloat16
        )

    def assemble(buf, seg, margin, reach, dilation):
        def line(at, left, middle, right):
            parts = []
            if PAD > reach:
                parts.append(jnp.zeros((PAD - reach, 128), jnp.float32))
            parts += [left.astype(jnp.float32), middle.astype(jnp.float32), right.astype(jnp.float32)]
            rest = width - PAD - tile_cols - reach
            if rest:
                parts.append(jnp.zeros((rest, 128), jnp.float32))
            spread(buf, at, 0, width, jnp.concatenate(parts, axis=0), dilation)

        def body_rows(i, carry):
            line(PAD + i, side[seg, 0, i, :reach, :], own[seg, i], side[seg, 1, i, :reach, :])
            return carry

        def cap_rows(i, carry):
            for which, first in ((0, PAD - margin), (1, PAD + tile_rows)):
                line(
                    first + i,
                    corner[seg, which, 0, i, :reach, :],
                    cap[seg, which, i],
                    corner[seg, which, 1, i, :reach, :],
                )
            return carry

        lax.fori_loop(0, tile_rows, body_rows, 0, unroll=2)
        lax.fori_loop(0, margin, cap_rows, 0)

    def layer(k, src, dilation, margin, finish, masked):
        copies[2 * k].wait()
        copies[2 * k + 1].wait()
        start = (PAD - margin) // 16 * 16
        stop = round_up(PAD + tile_cols + margin, 16)
        span = stop - start
        out_rows = tile_rows + 2 * margin
        first = PAD - margin
        blocks = -(-out_rows // (2 * dilation))
        chunk = max(
            n for n in range(1, blocks + 1)
            if blocks % n == 0 and (n == 1 or n * dilation * span <= CHUNK_ROWS)
        )
        bias = bias_ref[pl.ds(k, 1), :]
        if masked:
            col_pos = lax.broadcasted_iota(jnp.int32, (span, 128), 0) + (start - PAD) + col_start
            col_ok = jnp.logical_and(col_pos >= 0, col_pos < tile_cols * cols_n)
            col_scale = jnp.where(col_ok, 1.0, 0.0).astype(jnp.float32)

        def step(c, carry):
            base = first + c * (chunk * 2 * dilation)
            tops = [base + 2 * dilation * b + i for b in range(chunk) for i in range(dilation)]
            lhs = jnp.concatenate(
                [
                    jnp.concatenate(
                        [
                            acts[src, kx, top + (j - 1) * dilation, pl.ds(start, span), :]
                            for j in range(4)
                            for kx in range(3)
                        ],
                        axis=1,
                    )
                    for top in tops
                ],
                axis=0,
            )
            summed = jnp.dot(
                lhs, taps[k].reshape(12 * 128, 256), preferred_element_type=jnp.float32
            )
            for n, top in enumerate(tops):
                for o in range(2):
                    at = top + o * dilation
                    offset = n // dilation * 2 * dilation + n % dilation + o * dilation
                    if blocks == chunk and offset >= out_rows:
                        continue
                    value = summed[n * span : (n + 1) * span, o * 128 : (o + 1) * 128]
                    value = jnp.maximum(value + bias, 0.0)
                    if masked:
                        pos = at - PAD + row_start
                        inside = jnp.logical_and(pos >= 0, pos < tile_rows * rows_n)
                        value = value * (col_scale * jnp.where(inside, 1.0, 0.0))
                    finish(at, start, span, value)
            return carry

        if blocks == chunk:
            step(0, 0)
        else:
            lax.fori_loop(0, blocks // chunk, step, 0)

    seg = 0
    own_slot = 0
    for g in range(groups):
        group_slot = own_slot
        for which, members in enumerate(plan):
            margin = sum(2**l for l in members)
            reach = round_up(margin, 8)
            stage_edges(own_slot, margin, reach)
            if seg == 0:
                count = sum(
                    [jnp.where(exists(dr, dc), 1, 0) for dr, dc in neighbours()]
                    + [jnp.where(same, 0, 1) for _, _, same in partners]
                )
                pl.semaphore_wait(barrier, count)
            send_halo(own_slot, margin, reach)
            wait_halo(own_slot, margin, reach)
            buf = 0
            assemble(buf, own_slot, margin, reach, 2 ** members[0])
            left = margin
            for n, l in enumerate(members):
                left -= 2**l
                last = n == len(members) - 1
                if not last:
                    def finish(at, start, span, value, buf=buf, nxt=2 ** members[n + 1]):
                        spread(1 - buf, at, start, span, value, nxt)
                elif which < len(plan) - 1:
                    def finish(at, start, span, value, dst=own_slot + 1):
                        own[dst, at - PAD] = value[PAD - start : PAD - start + tile_cols].astype(
                            jnp.bfloat16
                        )
                else:
                    def finish(at, start, span, value, src=group_slot, dst=own_slot + 1):
                        hidden = value[PAD - start : PAD - start + tile_cols].astype(jnp.bfloat16)
                        section = own[src, at - PAD].astype(jnp.float32) + hidden.astype(jnp.float32)
                        own[dst, at - PAD] = section.astype(jnp.bfloat16)
                layer(g * layers + l, buf, 2**l, left, finish, masked=not last)
                buf = 1 - buf
            wait_sent(own_slot, margin, reach)
            own_slot += 1
            seg += 1

    final = own_slot
    my_block = row % ratio

    def mirror_copy(s):
        peer_row, peer_col, _ = partners[s]
        return pltpu.make_async_remote_copy(
            src_ref=mir_send.at[s],
            dst_ref=mir_recv.at[my_block],
            send_sem=mir_sems.at[s],
            recv_sem=mir_rsems.at[my_block],
            device_id={"row": peer_row, "col": peer_col},
            device_id_type=MESH,
        )

    value = own[final].astype(jnp.float32)
    for s in range(ratio):
        mir_send[s] = value[:, s * tile_rows : (s + 1) * tile_rows, :].astype(jnp.bfloat16)
        same = partners[s][2]

        @pl.when(jnp.logical_not(same))
        def _():
            mirror_copy(s).start()

        @pl.when(same)
        def _():
            cp = pltpu.make_async_copy(mir_send.at[s], mir_recv.at[my_block], mir_local)
            cp.start()
            cp.wait()
    for s in range(ratio):
        same = partners[s][2]

        @pl.when(jnp.logical_not(same))
        def _():
            pltpu.make_async_remote_copy(
                src_ref=mir_send.at[s],
                dst_ref=mir_recv.at[s],
                send_sem=mir_sems.at[s],
                recv_sem=mir_rsems.at[s],
                device_id={"row": partners[s][0], "col": partners[s][1]},
                device_id_type=MESH,
            ).wait_recv()
            mirror_copy(s).wait_send()
        flipped = jnp.transpose(mir_recv[s].astype(jnp.float32), (1, 0, 2))
        mine = own[final, :, pl.ds(s * tile_rows, tile_rows), :].astype(jnp.float32)
        out_ref[:, pl.ds(s * tile_rows, tile_rows), :] = (0.5 * (mine + flipped)).astype(jnp.bfloat16)


def solution(mesh):
    rows_n = mesh.shape["row"]
    cols_n = mesh.shape["col"]

    def body(input_map, conv_weights, conv_bias):
        tile_rows, tile_cols, channels = input_map.shape
        groups, layers = conv_weights.shape[:2]
        plan = SEGMENTS
        slots = groups * len(plan) + 1
        margin = max(sum(2**l for l in members) for members in plan)
        reach = round_up(margin, 8)
        ratio = rows_n // cols_n
        rows_held = tile_rows + 2 * PAD + 16
        width = round_up(tile_cols + 2 * PAD, 16)
        bf16 = jnp.bfloat16
        kernel = functools.partial(
            trunk, (groups, layers, tile_rows, tile_cols), plan, rows_n, cols_n
        )
        return pl.pallas_call(
            kernel,
            out_shape=jax.ShapeDtypeStruct(input_map.shape, bf16),
            in_specs=[
                pl.BlockSpec(memory_space=pl.ANY),
                pl.BlockSpec(memory_space=pl.ANY),
                pl.BlockSpec(memory_space=pltpu.VMEM),
            ],
            out_specs=pl.BlockSpec(memory_space=pltpu.VMEM),
            scratch_shapes=[
                pltpu.VMEM((groups * layers, 4, 3, channels, 2 * channels), bf16),
                pltpu.VMEM((2, 3, rows_held, width, channels), bf16),
                pltpu.VMEM((slots, tile_rows, tile_cols, channels), bf16),
                pltpu.VMEM((slots, 2, tile_rows, reach, channels), bf16),
                pltpu.VMEM((slots, 2, tile_rows, reach, channels), bf16),
                pltpu.VMEM((slots, 2, margin, tile_cols, channels), bf16),
                pltpu.VMEM((slots, 2, 2, margin, reach, channels), bf16),
                pltpu.VMEM((ratio, tile_rows, tile_rows, channels), bf16),
                pltpu.VMEM((ratio, tile_rows, tile_rows, channels), bf16),
                pltpu.SemaphoreType.DMA((groups * layers, 2)),
                pltpu.SemaphoreType.DMA,
                pltpu.SemaphoreType.DMA((slots, 9)),
                pltpu.SemaphoreType.DMA((slots, 9)),
                pltpu.SemaphoreType.DMA((ratio,)),
                pltpu.SemaphoreType.DMA((ratio,)),
                pltpu.SemaphoreType.DMA,
            ],
            compiler_params=pltpu.CompilerParams(
                collective_id=0, has_side_effects=True, vmem_limit_bytes=60 * 1024 * 1024
            ),
        )(input_map, conv_weights, conv_bias.reshape(groups * layers, channels))

    return jax.shard_map(
        body,
        mesh=mesh,
        in_specs=(P(("locus", "row"), "col", None), P(), P()),
        out_specs=P(("locus", "row"), "col", None),
        check_vma=False,
    )
```

time: 100 us -> 40 us (0.40)
  the two profiles are of different devices: /device:TPU:0 before, /device:TPU:6 now
where the time goes in v1:
time: 40 us; the launch traced here: 39.9 us
  Pallas kernels  38.3 us (96%)
  local copies, waits for them, and re-layouts  1.59 us (4%)
    pallas_call x1, Pallas kernels, body(): pl.pallas_call(kernel, out_shape=jax.ShapeDtypeStruct(input_map.shape, bf...  38.3 us
    unnamed x1, local copies, waits for them, and re-layouts  1.59 us

profile of v1, /device:TPU:6, one launch (start us, length us, event | category | flops | bytes accessed | tf_op | source)
XLA Modules:
  0.0 39.9 jit_solution(15900196889890348057)
XLA Ops:
  0.0 38.3 %shard_map.37 = bf16[24,24,128]{2,1,0:T(8,128)(2,1)} custom-call(bf16[24,24,128]{2,1,0:T(8,128)(2,1)} %input_ref.1, bf16[2,4,3,3,128,128]{5,4,3,2,1,0:T(8,128)(2,1)} %weight_ref.1, f32[8,128]{1,0:T(8,128)} %bitcast.1), custom_call_target="tpu_custom_call" | custom-call | tf_op jit(solution)/shard_map/pallas_call | solution.py:348
  38.3 1.6 %copy.5 = bf16[24,24,128]{2,1,0:T(8,128)(2,1)} copy(bf16[24,24,128]{2,1,0:T(8,128)(2,1)} %shard_map.37) | data formatting | bytes 294912

commit v2 on v1

--- a/solution.py
+++ b/solution.py
@@ -9,7 +9,8 @@
 
 SEGMENTS = ((0, 1, 2, 3),)
 PAD = 16
-CHUNK_ROWS = 832
+CHUNK_ROWS = 1664
+SUB = 13
 MESH = pl.DeviceIdType.MESH
 
 
@@ -28,14 +29,16 @@
 def trunk(
     shape, plan, rows_n, cols_n,
     input_ref, weight_ref, bias_ref, out_ref,
-    taps, acts, own, edge, side, cap, corner, mir_send, mir_recv,
+    taps, acts_a, acts_b, own, edge, side, cap, corner, mir_send, mir_recv,
     weight_sem, input_sem, halo_send, halo_recv, mir_sems, mir_rsems, mir_local,
+    detour, detour_send, detour_recv, onward_send, onward_recv,
 ):
     groups, layers, tile_rows, tile_cols = shape
     ratio = rows_n // cols_n
     row = lax.axis_index("row")
     col = lax.axis_index("col")
-    width = acts.shape[3]
+    acts = (acts_a, acts_b)
+    width = acts_a.shape[2]
     row_start = row * tile_rows
     col_start = col * tile_cols
 
@@ -75,7 +78,41 @@
         same = jnp.logical_and(peer_row == row, peer_col == col)
         partners.append((peer_row, peer_col, same))
 
+    direct_rows = tile_rows * 14 // 24
+    cuts = [direct_rows + (tile_rows - direct_rows) * n // 2 for n in range(2 + 1)]
+    pieces = list(zip(cuts[:-1], cuts[1:]))
+
+    def far(r, c, peer_r, peer_c):
+        return jnp.logical_and(r // 2 != peer_r // 2, c != peer_c)
+
+    def between(r, c, peer_r, peer_c):
+        return peer_r // 2 * 2 + r % 2, c
+
+    flows = []
+    for y in range(rows_n // 2):
+        for s in range(ratio):
+            src_row = 2 * y + row % 2
+            to_row, to_col = ratio * col + s, src_row // ratio
+            ok = jnp.logical_and(far(src_row, col, to_row, to_col), to_row // 2 == row // 2)
+            flows.append((y, s, (src_row, col), (to_row, to_col), src_row % ratio, ok))
+    my_slot = row // 2
+
+    def at_device(place):
+        return {"row": place[0], "col": place[1]}
+
     barrier = pltpu.get_barrier_semaphore()
+    for _, _, source, _, _, ok in flows:
+        @pl.when(ok)
+        def _():
+            pl.semaphore_signal(barrier, inc=1, device_id=at_device(source), device_id_type=MESH)
+    fars = [far(row, col, peer_row, peer_col) for peer_row, peer_col, _ in partners]
+    for (peer_row, peer_col, _), ok in zip(partners, fars):
+        @pl.when(ok)
+        def _():
+            pl.semaphore_signal(
+                barrier, inc=1, device_id=at_device(between(peer_row, peer_col, row, col)),
+                device_id_type=MESH,
+            )
     for dr, dc in neighbours():
         @pl.when(exists(dr, dc))
         def _():
@@ -87,7 +124,9 @@
                 barrier, inc=1, device_id={"row": peer_row, "col": peer_col}, device_id_type=MESH
             )
 
-    acts[...] = jnp.zeros_like(acts)
+    for buf in acts:
+        spare = (3, buf.shape[1] - PAD - tile_rows, width, 128)
+        buf[:, PAD + tile_rows :] = jnp.zeros(spare, jnp.bfloat16)
     taps[:, 3, :, :, 0:128] = jnp.zeros((groups * layers, 3, 128, 128), jnp.bfloat16)
     taps[:, 0, :, :, 128:256] = jnp.zeros((groups * layers, 3, 128, 128), jnp.bfloat16)
 
@@ -122,37 +161,77 @@
             device_id_type=MESH,
         )
 
+    def relayed(dr, dc):
+        inner = row % 2 == (0 if dr > 0 else 1)
+        return jnp.logical_and(exists(dr, dc), inner)
+
+    def straight(dr, dc):
+        if dr == 0 or dc == 0:
+            return exists(dr, dc)
+        inner = row % 2 == (0 if dr > 0 else 1)
+        return jnp.logical_and(exists(dr, dc), jnp.logical_not(inner))
+
+    def forward(seg, margin, reach, dr, dc):
+        rows = pl.ds(0, margin) if dr < 0 else pl.ds(tile_rows - margin, margin)
+        which = 0 if dc < 0 else 1
+        return pltpu.make_async_remote_copy(
+            src_ref=side.at[seg, which, rows, pl.ds(0, reach)],
+            dst_ref=corner.at[seg, 1 if dr < 0 else 0, which, pl.ds(0, margin), pl.ds(0, reach)],
+            send_sem=halo_send.at[seg, slot_of(dr, dc)],
+            recv_sem=halo_recv.at[seg, slot_of(-dr, dc)],
+            device_id=device(dr, 0),
+            device_id_type=MESH,
+        )
+
     def arrive(seg, margin, reach, dr, dc):
         transfer(seg, margin, reach, -dr, -dc).wait_recv()
 
     order = [(0, -1), (0, 1), (-1, 0), (1, 0), (-1, -1), (-1, 1), (1, -1), (1, 1)]
 
+    corners = order[4:]
+
     def send_halo(seg, margin, reach):
         for dr, dc in order:
+            @pl.when(straight(dr, dc))
+            def _():
+                transfer(seg, margin, reach, dr, dc).start()
+
+    def wait_halo(seg, margin, reach):
+        for dr, dc in order[:2]:
             @pl.when(exists(dr, dc))
             def _():
-                transfer(seg, margin, reach, dr, dc).start()
-
-    def wait_halo(seg, margin, reach):
-        for dr, dc in order:
-            @pl.when(exists(dr, dc))
-            def _():
                 arrive(seg, margin, reach, dr, dc)
+            for fr in (-1, 1):
+                @pl.when(relayed(fr, dc))
+                def _():
+                    forward(seg, margin, reach, fr, dc).start()
+        for dr, dc in order[2:]:
+            @pl.when(straight(dr, dc))
+            def _():
+                arrive(seg, margin, reach, dr, dc)
+        for dr, dc in corners:
+            @pl.when(relayed(dr, dc))
+            def _():
+                forward(seg, margin, reach, -dr, dc).wait_recv()
 
     def wait_sent(seg, margin, reach):
         for dr, dc in order:
-            @pl.when(exists(dr, dc))
+            @pl.when(straight(dr, dc))
             def _():
                 transfer(seg, margin, reach, dr, dc).wait_send()
-
-    def spread(buf, at, start, span, value, dilation):
-        acts[buf, 1, at, pl.ds(start, span), :] = value.astype(jnp.bfloat16)
-        acts[buf, 0, at, pl.ds(start, span), :] = pltpu.roll(value, dilation, 0).astype(jnp.bfloat16)
-        acts[buf, 2, at, pl.ds(start, span), :] = pltpu.roll(value, span - dilation, 0).astype(
-            jnp.bfloat16
-        )
-
-    def assemble(buf, seg, margin, reach, dilation):
+        for dr, dc in corners:
+            @pl.when(relayed(dr, dc))
+            def _():
+                forward(seg, margin, reach, dr, dc).wait_send()
+
+    def spread(buf, at, span, value, shifts):
+        for kx, shift in enumerate(shifts):
+            moved = pltpu.roll(value, value.shape[0] - shift, 0) if shift else value
+            acts[buf][kx, at, pl.ds(0, span), :] = moved[:span].astype(jnp.bfloat16)
+
+    def assemble(buf, seg, margin, reach, dilation, span):
+        first_col = PAD - margin
+
         def line(at, left, middle, right):
             parts = []
             if PAD > reach:
@@ -161,7 +240,8 @@
             rest = width - PAD - tile_cols - reach
             if rest:
                 parts.append(jnp.zeros((rest, 128), jnp.float32))
-            spread(buf, at, 0, width, jnp.concatenate(parts, axis=0), dilation)
+            shifts = [first_col + kx * dilation for kx in range(3)]
+            spread(buf, at, span, jnp.concatenate(parts, axis=0), shifts)
 
         def body_rows(i, carry):
             line(PAD + i, side[seg, 0, i, :reach, :], own[seg, i], side[seg, 1, i, :reach, :])
@@ -180,12 +260,13 @@
         lax.fori_loop(0, tile_rows, body_rows, 0, unroll=2)
         lax.fori_loop(0, margin, cap_rows, 0)
 
+    def span_of(margin):
+        return round_up(tile_cols + 2 * margin, 16)
+
     def layer(k, src, dilation, margin, finish, masked):
         copies[2 * k].wait()
         copies[2 * k + 1].wait()
-        start = (PAD - margin) // 16 * 16
-        stop = round_up(PAD + tile_cols + margin, 16)
-        span = stop - start
+        span = span_of(margin)
         out_rows = tile_rows + 2 * margin
         first = PAD - margin
         blocks = -(-out_rows // (2 * dilation))
@@ -195,43 +276,46 @@
         )
         bias = bias_ref[pl.ds(k, 1), :]
         if masked:
-            col_pos = lax.broadcasted_iota(jnp.int32, (span, 128), 0) + (start - PAD) + col_start
+            col_pos = lax.broadcasted_iota(jnp.int32, (span, 128), 0) + col_start - margin
             col_ok = jnp.logical_and(col_pos >= 0, col_pos < tile_cols * cols_n)
             col_scale = jnp.where(col_ok, 1.0, 0.0).astype(jnp.float32)
 
         def step(c, carry):
             base = first + c * (chunk * 2 * dilation)
             tops = [base + 2 * dilation * b + i for b in range(chunk) for i in range(dilation)]
-            lhs = jnp.concatenate(
-                [
-                    jnp.concatenate(
-                        [
-                            acts[src, kx, top + (j - 1) * dilation, pl.ds(start, span), :]
-                            for j in range(4)
-                            for kx in range(3)
-                        ],
-                        axis=1,
-                    )
-                    for top in tops
-                ],
-                axis=0,
-            )
-            summed = jnp.dot(
-                lhs, taps[k].reshape(12 * 128, 256), preferred_element_type=jnp.float32
-            )
-            for n, top in enumerate(tops):
-                for o in range(2):
-                    at = top + o * dilation
-                    offset = n // dilation * 2 * dilation + n % dilation + o * dilation
-                    if blocks == chunk and offset >= out_rows:
-                        continue
-                    value = summed[n * span : (n + 1) * span, o * 128 : (o + 1) * 128]
-                    value = jnp.maximum(value + bias, 0.0)
-                    if masked:
-                        pos = at - PAD + row_start
-                        inside = jnp.logical_and(pos >= 0, pos < tile_rows * rows_n)
-                        value = value * (col_scale * jnp.where(inside, 1.0, 0.0))
-                    finish(at, start, span, value)
+            parts = [tops[n : n + SUB] for n in range(0, len(tops), SUB)]
+            for part, group in enumerate(parts):
+                lhs = jnp.concatenate(
+                    [
+                        jnp.concatenate(
+                            [
+                                acts[src][kx, top + (j - 1) * dilation, pl.ds(0, span), :]
+                                for j in range(4)
+                                for kx in range(3)
+                            ],
+                            axis=1,
+                        )
+                        for top in group
+                    ],
+                    axis=0,
+                )
+                summed = jnp.dot(
+                    lhs, taps[k].reshape(12 * 128, 256), preferred_element_type=jnp.float32
+                )
+                for m, top in enumerate(group):
+                    n = part * SUB + m
+                    for o in range(2):
+                        at = top + o * dilation
+                        offset = n // dilation * 2 * dilation + n % dilation + o * dilation
+                        if blocks == chunk and offset >= out_rows:
+                            continue
+                        value = summed[m * span : (m + 1) * span, o * 128 : (o + 1) * 128]
+                        value = jnp.maximum(value + bias, 0.0)
+                        if masked:
+                            pos = at - PAD + row_start
+                            inside = jnp.logical_and(pos >= 0, pos < tile_rows * rows_n)
+                            value = value * (col_scale * jnp.where(inside, 1.0, 0.0))
+                        finish(at, value)
             return carry
 
         if blocks == chunk:
@@ -251,27 +335,31 @@
                 count = sum(
                     [jnp.where(exists(dr, dc), 1, 0) for dr, dc in neighbours()]
                     + [jnp.where(same, 0, 1) for _, _, same in partners]
+                    + [jnp.where(ok, 1, 0) for ok in fars]
+                    + [jnp.where(flow[-1], 1, 0) for flow in flows]
                 )
                 pl.semaphore_wait(barrier, count)
             send_halo(own_slot, margin, reach)
             wait_halo(own_slot, margin, reach)
             buf = 0
-            assemble(buf, own_slot, margin, reach, 2 ** members[0])
+            assemble(
+                buf, own_slot, margin, reach, 2 ** members[0], span_of(margin - 2 ** members[0])
+            )
             left = margin
             for n, l in enumerate(members):
                 left -= 2**l
                 last = n == len(members) - 1
                 if not last:
-                    def finish(at, start, span, value, buf=buf, nxt=2 ** members[n + 1]):
-                        spread(1 - buf, at, start, span, value, nxt)
+                    def finish(at, value, buf=buf, nxt=2 ** members[n + 1], margin=left):
+                        spread(1 - buf, at, span_of(margin - nxt), value, [0, nxt, 2 * nxt])
                 elif which < len(plan) - 1:
-                    def finish(at, start, span, value, dst=own_slot + 1):
-                        own[dst, at - PAD] = value[PAD - start : PAD - start + tile_cols].astype(
+                    def finish(at, value, dst=own_slot + 1):
+                        own[dst, at - PAD] = value[:tile_cols].astype(
                             jnp.bfloat16
                         )
                 else:
-                    def finish(at, start, span, value, src=group_slot, dst=own_slot + 1):
-                        hidden = value[PAD - start : PAD - start + tile_cols].astype(jnp.bfloat16)
+                    def finish(at, value, src=group_slot, dst=own_slot + 1):
+                        hidden = value[:tile_cols].astype(jnp.bfloat16)
                         section = own[src, at - PAD].astype(jnp.float32) + hidden.astype(jnp.float32)
                         own[dst, at - PAD] = section.astype(jnp.bfloat16)
                 layer(g * layers + l, buf, 2**l, left, finish, masked=not last)
@@ -283,14 +371,46 @@
     final = own_slot
     my_block = row % ratio
 
-    def mirror_copy(s):
-        peer_row, peer_col, _ = partners[s]
+    def mirror_copy(s, block, count):
         return pltpu.make_async_remote_copy(
-            src_ref=mir_send.at[s],
-            dst_ref=mir_recv.at[my_block],
+            src_ref=mir_send.at[s, pl.ds(0, count)],
+            dst_ref=mir_recv.at[block, pl.ds(0, count)],
             send_sem=mir_sems.at[s],
-            recv_sem=mir_rsems.at[my_block],
-            device_id={"row": peer_row, "col": peer_col},
+            recv_sem=mir_rsems.at[block],
+            device_id=at_device(partners[s][:2]),
+            device_id_type=MESH,
+        )
+
+    def to_between(s, n):
+        low, high = pieces[n]
+        return pltpu.make_async_remote_copy(
+            src_ref=mir_send.at[s, pl.ds(low, high - low)],
+            dst_ref=detour.at[my_slot, s, pl.ds(low - direct_rows, high - low)],
+            send_sem=detour_send.at[s, n],
+            recv_sem=detour_recv.at[my_slot, s, n],
+            device_id=at_device(between(row, col, *partners[s][:2])),
+            device_id_type=MESH,
+        )
+
+    def onward(slot, s, target, block, n):
+        low, high = pieces[n]
+        return pltpu.make_async_remote_copy(
+            src_ref=detour.at[slot, s, pl.ds(low - direct_rows, high - low)],
+            dst_ref=mir_recv.at[block, pl.ds(low, high - low)],
+            send_sem=onward_send.at[slot, s, n],
+            recv_sem=onward_recv.at[block, n],
+            device_id=at_device(target),
+            device_id_type=MESH,
+        )
+
+    def arrived_between(slot, s, source, n):
+        low, high = pieces[n]
+        return pltpu.make_async_remote_copy(
+            src_ref=mir_send.at[s, pl.ds(low, high - low)],
+            dst_ref=detour.at[slot, s, pl.ds(low - direct_rows, high - low)],
+            send_sem=detour_send.at[s, n],
+            recv_sem=detour_recv.at[slot, s, n],
+            device_id=at_device(source),
             device_id_type=MESH,
         )
 
@@ -298,33 +418,52 @@
     for s in range(ratio):
         mir_send[s] = value[:, s * tile_rows : (s + 1) * tile_rows, :].astype(jnp.bfloat16)
         same = partners[s][2]
-
-        @pl.when(jnp.logical_not(same))
-        def _():
-            mirror_copy(s).start()
+        near = jnp.logical_not(jnp.logical_or(same, fars[s]))
+
+        @pl.when(near)
+        def _():
+            mirror_copy(s, my_block, tile_rows).start()
+
+        @pl.when(fars[s])
+        def _():
+            for n in range(len(pieces)):
+                to_between(s, n).start()
+            mirror_copy(s, my_block, direct_rows).start()
 
         @pl.when(same)
         def _():
             cp = pltpu.make_async_copy(mir_send.at[s], mir_recv.at[my_block], mir_local)
             cp.start()
             cp.wait()
+    for n in range(len(pieces)):
+        for slot, s, source, target, block, ok in flows:
+            @pl.when(ok)
+            def _():
+                arrived_between(slot, s, source, n).wait_recv()
+                onward(slot, s, target, block, n).start()
     for s in range(ratio):
-        same = partners[s][2]
-
-        @pl.when(jnp.logical_not(same))
-        def _():
-            pltpu.make_async_remote_copy(
-                src_ref=mir_send.at[s],
-                dst_ref=mir_recv.at[s],
-                send_sem=mir_sems.at[s],
-                recv_sem=mir_rsems.at[s],
-                device_id={"row": partners[s][0], "col": partners[s][1]},
-                device_id_type=MESH,
-            ).wait_recv()
-            mirror_copy(s).wait_send()
+        near = jnp.logical_not(jnp.logical_or(partners[s][2], fars[s]))
+
+        @pl.when(near)
+        def _():
+            mirror_copy(s, s, tile_rows).wait_recv()
+            mirror_copy(s, my_block, tile_rows).wait_send()
+
+        @pl.when(fars[s])
+        def _():
+            mirror_copy(s, s, direct_rows).wait_recv()
+            mirror_copy(s, my_block, direct_rows).wait_send()
+            for n in range(len(pieces)):
+                onward(0, s, partners[s][:2], s, n).wait_recv()
+                to_between(s, n).wait_send()
         flipped = jnp.transpose(mir_recv[s].astype(jnp.float32), (1, 0, 2))
         mine = own[final, :, pl.ds(s * tile_rows, tile_rows), :].astype(jnp.float32)
         out_ref[:, pl.ds(s * tile_rows, tile_rows), :] = (0.5 * (mine + flipped)).astype(jnp.bfloat16)
+    for n in range(len(pieces)):
+        for slot, s, source, target, block, ok in flows:
+            @pl.when(ok)
+            def _():
+                onward(slot, s, target, block, n).wait_send()
 
 
 def solution(mesh):
@@ -356,7 +495,8 @@
             out_specs=pl.BlockSpec(memory_space=pltpu.VMEM),
             scratch_shapes=[
                 pltpu.VMEM((groups * layers, 4, 3, channels, 2 * channels), bf16),
-                pltpu.VMEM((2, 3, rows_held, width, channels), bf16),
+                pltpu.VMEM((3, rows_held, width, channels), bf16),
+                pltpu.VMEM((3, rows_held, width, channels), bf16),
                 pltpu.VMEM((slots, tile_rows, tile_cols, channels), bf16),
                 pltpu.VMEM((slots, 2, tile_rows, reach, channels), bf16),
                 pltpu.VMEM((slots, 2, tile_rows, reach, channels), bf16),
@@ -371,6 +511,11 @@
                 pltpu.SemaphoreType.DMA((ratio,)),
                 pltpu.SemaphoreType.DMA((ratio,)),
                 pltpu.SemaphoreType.DMA,
+                pltpu.VMEM((rows_n // 2, ratio, tile_rows, tile_rows, channels), bf16),
+                pltpu.SemaphoreType.DMA((ratio, 2)),
+                pltpu.SemaphoreType.DMA((rows_n // 2, ratio, 2)),
+                pltpu.SemaphoreType.DMA((rows_n // 2, ratio, 2)),
+                pltpu.SemaphoreType.DMA((ratio, 2)),
             ],
             compiler_params=pltpu.CompilerParams(
                 collective_id=0, has_side_effects=True, vmem_limit_bytes=60 * 1024 * 1024

time: 40 us -> 36.7 us (0.918)
  Pallas kernels: 38.3 us -> 34.9 us
    pallas_call x1, Pallas kernels: 38.3 us -> 34.9 us  [body(): pl.pallas_call(kernel, out_shape=jax.ShapeDtypeStruct(input_map.shape, bf...]
where the time goes in v2:
time: 36.7 us; the launch traced here: 36.5 us
  Pallas kernels  34.9 us (95%)
  local copies, waits for them, and re-layouts  1.59 us (4%)
    pallas_call x1, Pallas kernels, body(): pl.pallas_call(kernel, out_shape=jax.ShapeDtypeStruct(input_map.shape, bf...  34.9 us
    unnamed x1, local copies, waits for them, and re-layouts  1.59 us

profile of v2, /device:TPU:6, one launch (start us, length us, event | category | flops | bytes accessed | tf_op | source)
XLA Modules:
  0.0 36.5 jit_solution(13618948328370075487)
XLA Ops:
  0.0 34.9 %shard_map.37 = bf16[24,24,128]{2,1,0:T(8,128)(2,1)} custom-call(bf16[24,24,128]{2,1,0:T(8,128)(2,1)} %input_ref.1, bf16[2,4,3,3,128,128]{5,4,3,2,1,0:T(8,128)(2,1)} %weight_ref.1, f32[8,128]{1,0:T(8,128)} %bitcast.1), custom_call_target="tpu_custom_call" | custom-call | tf_op jit(solution)/shard_map/pallas_call | solution.py:487
  34.9 1.6 %copy.5 = bf16[24,24,128]{2,1,0:T(8,128)(2,1)} copy(bf16[24,24,128]{2,1,0:T(8,128)(2,1)} %shard_map.37) | data formatting | bytes 294912

commit v3 on v2

--- a/solution.py
+++ b/solution.py
@@ -78,7 +78,7 @@
         same = jnp.logical_and(peer_row == row, peer_col == col)
         partners.append((peer_row, peer_col, same))
 
-    direct_rows = tile_rows * 14 // 24
+    direct_rows = tile_rows * 16 // 24
     cuts = [direct_rows + (tile_rows - direct_rows) * n // 2 for n in range(2 + 1)]
     pieces = list(zip(cuts[:-1], cuts[1:]))
 

time: 36.7 us -> 36.1 us (0.984)
  Pallas kernels: 34.9 us -> 34.4 us
    pallas_call x1, Pallas kernels: 34.9 us -> 34.4 us  [body(): pl.pallas_call(kernel, out_shape=jax.ShapeDtypeStruct(input_map.shape, bf...]
where the time goes in v3:
time: 36.1 us; the launch traced here: 36 us
  Pallas kernels  34.4 us (95%)
  local copies, waits for them, and re-layouts  1.59 us (4%)
    pallas_call x1, Pallas kernels, body(): pl.pallas_call(kernel, out_shape=jax.ShapeDtypeStruct(input_map.shape, bf...  34.4 us
    unnamed x1, local copies, waits for them, and re-layouts  1.59 us

profile of v3, /device:TPU:6, one launch (start us, length us, event | category | flops | bytes accessed | tf_op | source)
XLA Modules:
  0.0 36.0 jit_solution(16291749818865941881)
XLA Ops:
  0.0 34.4 %shard_map.37 = bf16[24,24,128]{2,1,0:T(8,128)(2,1)} custom-call(bf16[24,24,128]{2,1,0:T(8,128)(2,1)} %input_ref.1, bf16[2,4,3,3,128,128]{5,4,3,2,1,0:T(8,128)(2,1)} %weight_ref.1, f32[8,128]{1,0:T(8,128)} %bitcast.1), custom_call_target="tpu_custom_call" | custom-call | tf_op jit(solution)/shard_map/pallas_call | solution.py:487
  34.4 1.6 %copy.5 = bf16[24,24,128]{2,1,0:T(8,128)(2,1)} copy(bf16[24,24,128]{2,1,0:T(8,128)(2,1)} %shard_map.37) | data formatting | bytes 294912
